TPU v7x, 512 devices: a whole 4x8x8 slice. The times are simulated.
512 devices in a mesh: wide: 64 (over z, y), rows: 8 (over x, core).
Axes of the slice: x: 4, y: 8, z: 8, core: 2. Of those that a mesh axis runs over, the one named last changes fastest.
Arguments:
- slabs: bfloat16 [64, 8, 10, 32, 128], P('wide', 'rows'), may hold values from -6 to 6
- dest: int32 [64, 8, 10], P('wide', 'rows'), may hold values from 0 to 63, as said below
- pos: int32 [64, 8, 10], P('wide', 'rows'), may hold values from 0 to 9, as said below
- lengths: int32 [64], P('wide'), may hold values from 1 to 5
- cot: bfloat16 [64, 5, 16, 32, 128], P('wide', None, 'rows'), may hold values from -6 to 6
- w_first: bfloat16 [3456, 128], P('wide'), may hold values from -0.109375 to 0.109375
- w_second: bfloat16 [3456, 128], P('wide'), may hold values from -0.109375 to 0.109375
Outputs:
- block_out: bfloat16 [64, 5, 16, 32, 128], P('wide', None, 'rows')
- grad_input: bfloat16 [64, 5, 16, 32, 128], P('wide', None, 'rows')
- grad_w_first: float32 [3456, 128], P('wide')
- grad_w_second: float32 [3456, 128], P('wide')
Inputs may be any that keep to these rules, and one draw needn't show every extreme that they name: `dest`: within a band no loader sends more than one slab to any clip; every clip receives exactly 10 slabs in each band. `pos`: for every clip and band the 10 slabs it receives carry the places 0 to 9, each once.
All inputs are finite; a program needn't handle non-finite values.
Results may differ from a plain program's by a relative error of at most 0.018.
Values may be sent and summed in bfloat16 or wider, within the bound.
A program may use at most 64 MiB of HBM per device.

v0:
```python
import math
import jax
import jax.numpy as jnp
from jax import lax
from jax.sharding import PartitionSpec as P


def with_halo(block, sides, width):
    for axis, dim in sides:
        count = lax.axis_size(axis)
        forward = [(i, i + 1) for i in range(count - 1)]
        backward = [(target, source) for source, target in forward]
        low = lax.ppermute(
            lax.slice_in_dim(block, block.shape[dim] - width, None, axis=dim), axis, forward
        )
        high = lax.ppermute(lax.slice_in_dim(block, 0, width, axis=dim), axis, backward)
        block = jnp.concatenate([low, block, high], axis=dim)
    return block


def silu_slope(values):
    sig = jax.nn.sigmoid(values)
    return sig * (1.0 + values * (1.0 - sig))


def conv_forward(extended, kernel):
    padded = jnp.concatenate([extended[:1], extended[:1], extended], axis=0)
    result = lax.conv_general_dilated(
        padded[None],
        kernel,
        (1, 1, 1),
        ((0, 0), (0, 0), (1, 1)),
        dimension_numbers=("NDHWC", "DHWIO", "NDHWC"),
        preferred_element_type=jnp.float32,
    )
    return result[0]


def conv_weight_grad(extended, upstream):
    padded = jnp.concatenate([extended[:1], extended[:1], extended], axis=0)
    result = lax.conv_general_dilated(
        padded[None],
        upstream[None],
        (1, 1, 1),
        ((0, 0), (0, 0), (1, 1)),
        dimension_numbers=("CDHWN", "IDHWO", "NDHWC"),
        preferred_element_type=jnp.float32,
    )
    channels = extended.shape[-1]
    return jnp.transpose(result, (1, 2, 3, 0, 4)).reshape(27 * channels, upstream.shape[-1])


def conv_data_grad(upstream_ext, kernel):
    padded = jnp.pad(upstream_ext, ((2, 2), (0, 0), (0, 0), (0, 0)))
    flipped = kernel[::-1, ::-1, ::-1]
    result = lax.conv_general_dilated(
        padded[None],
        flipped,
        (1, 1, 1),
        ((0, 0), (0, 0), (1, 1)),
        dimension_numbers=("NDHWC", "DHWOI", "NDHWC"),
        preferred_element_type=jnp.float32,
    )[0]
    head = (result[0] + result[1] + result[2])[None]
    return jnp.concatenate([head, result[3:]], axis=0)


def body(slabs, dest, pos, lengths, cot, w_first, w_second):
    wide_size = lax.axis_size("wide")
    band_count = lax.axis_size("rows")
    slab_count = slabs.shape[2]
    columns = slabs.shape[3]
    channels = slabs.shape[4]
    frames = cot.shape[1]
    band_rows = cot.shape[2]
    capacity = -(-slab_count // wide_size)
    slot_count = wide_size * capacity
    targets = dest[0, 0]
    places = pos[0, 0]
    ranking = jnp.arange(slab_count, dtype=jnp.int32)
    earlier = (targets[None, :] == targets[:, None]) & (ranking[None, :] < ranking[:, None])
    slab_rank = jnp.sum(earlier.astype(jnp.int32), axis=1)
    slot_of = targets * capacity + slab_rank
    placing = slot_of[None, :] == jnp.arange(slot_count, dtype=jnp.int32)[:, None]
    flat_slabs = slabs[0, 0].reshape(slab_count, columns * channels)
    outgoing = jnp.dot(placing.astype(jnp.bfloat16), flat_slabs, preferred_element_type=jnp.float32)
    outgoing = outgoing.astype(jnp.bfloat16).reshape(wide_size, capacity, columns * channels)
    labels = jnp.sum(jnp.where(placing, places[None, :] + 1, 0), axis=1) - 1
    labels = labels.reshape(wide_size, capacity)
    arrived, arrived_places = (
        lax.all_to_all(outgoing, "wide", split_axis=0, concat_axis=0, tiled=True),
        lax.all_to_all(labels, "wide", split_axis=0, concat_axis=0, tiled=True),
    )
    settle = (
        arrived_places.reshape(slot_count)[None, :]
        == jnp.arange(slab_count, dtype=jnp.int32)[:, None]
    )
    tile = jnp.dot(
        settle.astype(jnp.bfloat16),
        arrived.reshape(slot_count, columns * channels),
        preferred_element_type=jnp.float32,
    )
    tile = tile.astype(jnp.bfloat16).reshape(frames, band_rows, columns, channels)
    full_first, full_second = (
        lax.all_gather(w_first, "wide", axis=0, tiled=True),
        lax.all_gather(w_second, "wide", axis=0, tiled=True),
    )
    kernel_first = full_first.reshape(3, 3, 3, channels, channels)
    kernel_second = full_second.reshape(3, 3, 3, channels, channels)
    tile_wide = tile.astype(jnp.float32)
    first = jax.nn.silu(tile_wide).astype(jnp.bfloat16)
    first_ext = with_halo(first, (("rows", 1),), 1)
    act = conv_forward(first_ext, kernel_first).astype(jnp.bfloat16)
    second = jax.nn.silu(act.astype(jnp.float32)).astype(jnp.bfloat16)
    second_ext = with_halo(second, (("rows", 1),), 1)
    block_out = (tile_wide + conv_forward(second_ext, kernel_second)).astype(jnp.bfloat16)
    live = (jnp.arange(frames, dtype=jnp.int32) < lengths[0])[:, None, None, None]
    out_grad = jnp.where(live, cot[0], jnp.zeros_like(cot[0]))
    out_grad_ext = with_halo(out_grad, (("rows", 1),), 1)
    weight_second = conv_weight_grad(second_ext, out_grad)
    hidden_grad = conv_data_grad(out_grad_ext, kernel_second)
    act_grad = (hidden_grad * silu_slope(act.astype(jnp.float32))).astype(jnp.bfloat16)
    act_grad_ext = with_halo(act_grad, (("rows", 1),), 1)
    weight_first = conv_weight_grad(first_ext, act_grad)
    first_grad = conv_data_grad(act_grad_ext, kernel_first)
    grad_input = (out_grad.astype(jnp.float32) + first_grad * silu_slope(tile_wide)).astype(
        jnp.bfloat16
    )
    scale = 1.0 / math.sqrt(frames * band_rows * columns * band_count * wide_size)
    weight_first = weight_first * scale
    weight_second = weight_second * scale
    total_first, total_second = (
        lax.psum(weight_first.astype(jnp.bfloat16), "rows").astype(jnp.float32),
        lax.psum(weight_second.astype(jnp.bfloat16), "rows").astype(jnp.float32),
    )
    share_first, share_second = (
        lax.psum_scatter(total_first, "wide", scatter_dimension=0, tiled=True),
        lax.psum_scatter(total_second, "wide", scatter_dimension=0, tiled=True),
    )
    return (block_out[None], grad_input[None], share_first, share_second)


def solution(mesh):
    return jax.shard_map(
        body,
        mesh=mesh,
        in_specs=(
            P("wide", "rows", None, None, None),
            P("wide", "rows", None),
            P("wide", "rows", None),
            P("wide"),
            P("wide", None, "rows", None, None),
            P("wide", None),
            P("wide", None),
        ),
        out_specs=(
            P("wide", None, "rows", None, None),
            P("wide", None, "rows", None, None),
            P("wide", None),
            P("wide", None),
        ),
        check_vma=False,
    )
```

profile of v0, /device:TPU:24, one launch (start us, length us, event | category | flops | bytes accessed | tf_op | source)
XLA Modules:
  0.0 527.8 jit_solution(5221411180850742156)
XLA Ops:
  10.2 16.4 %all-to-all-start = ((s32[64,1,1]{2,1,0:T(1,128)}), s32[64,1,1]{2,1,0:T(1,128)S(1)}, u32[]{:S(2)}, u32[]{:S(2)}) async-start(s32[64,1,1]{2,1,0:T(1,128)} %copy.172), calls=%async_computation | async-start | bytes 65536 | tf_op jit(solution)/shard_map/all_to_all | solution.py:92
  32.3 3.5 all-to-all-done
  35.8 9.2 %all-to-all-start.1 = ((bf16[64,2,2048]{2,1,0:T(2,128)(2,1)}), bf16[64,2,2048]{2,1,0:T(2,128)(2,1)S(1)}, u32[]{:S(2)}, u32[]{:S(2)}) async-start(bf16[64,2,2048]{2,1,0:T(2,128)(2,1)} %reshape.276), calls=%async_computation.1 | async-start | bytes 1048576 | tf_op jit(solution)/shard_map/all_to_all | solution.py:91
  49.4 52.7 %all-gather = bf16[64,54,128]{2,1,0:T(8,128)(2,1)S(1)} all-gather(bf16[1,54,128]{2,1,0:T(8,128)(2,1)S(1)} %bitcast.138), channel_id=1, replica_groups=mesh['wide'=64,'rows'=8] {'wide'}, dimensions={0}, use_global_device_ids=true | all-gather | bytes 898560 | tf_op jit(solution)/shard_map/all_gather | solution.py:105
  102.1 48.3 %all-gather.1 = bf16[64,54,128]{2,1,0:T(8,128)(2,1)S(1)} all-gather(bf16[1,54,128]{2,1,0:T(8,128)(2,1)S(1)} %bitcast.139), channel_id=1, replica_groups=mesh['wide'=64,'rows'=8] {'wide'}, dimensions={0}, use_global_device_ids=true | all-gather | bytes 898560 | tf_op jit(solution)/shard_map/all_gather | solution.py:106
  164.1 3.8 collective-permute-start.6
  169.3 5.0 collective-permute-start.2
  174.5 3.5 multiply_convert_fusion.1
  182.0 3.5 multiply_convert_fusion
  185.6 74.2 %all-reduce.10.cloned.1.call-done = (bf16[3456,128]{1,0:T(8,128)(2,1)}, bf16[3456,128]{1,0:T(8,128)(2,1)}) async-done(((bf16[3456,128]{1,0:T(8,128)(2,1)}, bf16[3456,128]{1,0:T(8,128)(2,1)}), (bf16[3456,128]{1,0:T(8,128)(2,1)}, bf16[3456,128]{1,0:T(8,128)(2,1)})) %all-reduce.10.cloned.1.call-update) | async-done | bytes 1769488 | tf_op jit(solution)/shard_map/psum | solution.py:133
  261.3 162.5 %fusion.84 = (f32[64,128]{1,0:T(8,128)}, f32[64,128]{1,0:T(8,128)}) fusion(f32[3456,128]{1,0:T(8,128)S(1)} %convert_element_type.113, f32[3456,128]{1,0:T(8,128)S(1)} %convert_element_type.116), kind=kCustom, calls=%all-reduce-scatter.2 | all-reduce-scatter fusion | flops 1048577 | bytes 3606528
  426.4 4.0 collective-permute-start.14
  431.2 11.2 %collective-permute-start.13 = (f32[64,128]{1,0:T(8,128)}, f32[64,128]{1,0:T(8,128)S(1)}, u32[]{:S(2)}, u32[]{:S(2)}) collective-permute-start(f32[64,128]{1,0:T(8,128)} %get-tuple-element.28), channel_id=1, source_target_pairs={{0,48},{8,56},{16,64},{24,72},{32,80},{40,88},{48,96},{56,104},{64... | collective-permute-start | bytes 98312
  446.6 4.9 collective-permute-start.12
  451.6 9.5 %collective-permute-start.11 = (f32[64,128]{1,0:T(8,128)}, f32[64,128]{1,0:T(8,128)S(1)}, u32[]{:S(2)}, u32[]{:S(2)}) collective-permute-start(f32[64,128]{1,0:T(8,128)} %get-tuple-element.28), channel_id=1, source_target_pairs={{0,32},{8,40},{16,48},{24,56},{32,64},{40,72},{48,80},{56,88},{64,... | collective-permute-start | bytes 98312
  461.1 3.2 collective-permute-start.10
  464.3 7.9 %collective-permute-start.9 = (f32[64,128]{1,0:T(8,128)}, f32[64,128]{1,0:T(8,128)S(1)}, u32[]{:S(2)}, u32[]{:S(2)}) collective-permute-start(f32[64,128]{1,0:T(8,128)} %get-tuple-element.28), channel_id=1, source_target_pairs={{0,16},{8,24},{16,32},{24,40},{32,48},{40,56},{48,64},{56,72},{64,... | collective-permute-start | bytes 98312
  475.5 3.5 collective-permute-start.25
  479.0 3.4 collective-permute-start.24
  482.4 3.1 collective-permute-start.23
  486.3 4.0 collective-permute-start.27
  495.9 7.8 %collective-permute-start.21 = (f32[64,128]{1,0:T(8,128)}, f32[64,128]{1,0:T(8,128)S(1)}, u32[]{:S(2)}, u32[]{:S(2)}) collective-permute-start(f32[64,128]{1,0:T(8,128)} %get-tuple-element.29), channel_id=1, source_target_pairs={{0,32},{8,40},{16,48},{24,56},{32,64},{40,72},{48,80},{56,88},{64,... | collective-permute-start | bytes 98312
  506.2 5.9 %collective-permute-start.19 = (f32[64,128]{1,0:T(8,128)}, f32[64,128]{1,0:T(8,128)S(1)}, u32[]{:S(2)}, u32[]{:S(2)}) collective-permute-start(f32[64,128]{1,0:T(8,128)} %get-tuple-element.29), channel_id=1, source_target_pairs={{0,16},{8,24},{16,32},{24,40},{32,48},{40,56},{48,64},{56,72},{64,... | collective-permute-start | bytes 98312
  514.6 3.4 collective-permute-done.18
  (142 shorter events, 57.1 us)
Async XLA Ops:
  10.2 25.6 %all-to-all-start = ((s32[64,1,1]{2,1,0:T(1,128)}), s32[64,1,1]{2,1,0:T(1,128)S(1)}, u32[]{:S(2)}, u32[]{:S(2)}) async-start(s32[64,1,1]{2,1,0:T(1,128)} %copy.172), calls=%async_computation | async-start | bytes 65536 | tf_op jit(solution)/shard_map/all_to_all | solution.py:92
  35.8 118.8 %all-to-all-start.1 = ((bf16[64,2,2048]{2,1,0:T(2,128)(2,1)}), bf16[64,2,2048]{2,1,0:T(2,128)(2,1)S(1)}, u32[]{:S(2)}, u32[]{:S(2)}) async-start(bf16[64,2,2048]{2,1,0:T(2,128)(2,1)} %reshape.276), calls=%async_computation.1 | async-start | bytes 1048576 | tf_op jit(solution)/shard_map/all_to_all | solution.py:91
  45.0 214.7 %all-reduce.10.cloned.1.call-start = ((), (), s32[]{:S(2)}) async-start(), calls=%async_computation.2 | async-start | bytes 3538944 | tf_op jit(solution)/shard_map/psum | solution.py:133
  45.1 107.9 %collective-permute-start.5 = (bf16[5,1,32,128]{3,2,1,0:T(8,128)(2,1)S(1)}, bf16[5,1,32,128]{3,2,1,0:T(8,128)(2,1)S(1)}, u32[]{:S(2)}, u32[]{:S(2)}) collective-permute-start(bf16[5,1,32,128]{3,2,1,0:T(8,128)(2,1)S(1)} %get-tuple-element.44), channel_id=1, source_target_pairs={{1,0},{2,1},{3,2},{4,3},{5,4},{6,5},{7,6},{9,8},{10,9},{11,10},{12... | collective-permute-start | bytes 122888 | tf_op jit(solution)/shard_map/ppermute | solution.py:16
  46.4 106.6 %collective-permute-start.4 = (bf16[5,1,32,128]{3,2,1,0:T(8,128)(2,1)S(1)}, bf16[5,1,32,128]{3,2,1,0:T(8,128)(2,1)S(1)}, u32[]{:S(2)}, u32[]{:S(2)}) collective-permute-start(bf16[5,1,32,128]{3,2,1,0:T(8,128)(2,1)S(1)} %get-tuple-element.43), channel_id=1, source_target_pairs={{0,1},{1,2},{2,3},{3,4},{4,5},{5,6},{6,7},{8,9},{9,10},{10,11},{11... | collective-permute-start | bytes 122888 | tf_op jit(solution)/shard_map/ppermute | solution.py:13
  162.8 15.1 %collective-permute-start.7 = (bf16[5,1,32,128]{3,2,1,0:T(8,128)(2,1)S(1)}, bf16[5,1,32,128]{3,2,1,0:T(8,128)(2,1)S(1)}, u32[]{:S(2)}, u32[]{:S(2)}) collective-permute-start(bf16[5,1,32,128]{3,2,1,0:T(8,128)(2,1)S(1)} %get-tuple-element.40), channel_id=1, source_target_pairs={{1,0},{2,1},{3,2},{4,3},{5,4},{6,5},{7,6},{9,8},{10,9},{11,10},{12... | collective-permute-start | bytes 122888 | tf_op jit(solution)/shard_map/ppermute | solution.py:16
  164.1 13.8 %collective-permute-start.6 = (bf16[5,1,32,128]{3,2,1,0:T(8,128)(2,1)S(1)}, bf16[5,1,32,128]{3,2,1,0:T(8,128)(2,1)S(1)}, u32[]{:S(2)}, u32[]{:S(2)}) collective-permute-start(bf16[5,1,32,128]{3,2,1,0:T(8,128)(2,1)S(1)} %get-tuple-element.39), channel_id=1, source_target_pairs={{0,1},{1,2},{2,3},{3,4},{4,5},{5,6},{6,7},{8,9},{9,10},{10,11},{11... | collective-permute-start | bytes 122888 | tf_op jit(solution)/shard_map/ppermute | solution.py:13
  168.0 11.9 %collective-permute-start.3 = (bf16[5,1,32,128]{3,2,1,0:T(8,128)(2,1)S(1)}, bf16[5,1,32,128]{3,2,1,0:T(8,128)(2,1)S(1)}, u32[]{:S(2)}, u32[]{:S(2)}) collective-permute-start(bf16[5,1,32,128]{3,2,1,0:T(8,128)(2,1)S(1)} %get-tuple-element.46), channel_id=1, source_target_pairs={{1,0},{2,1},{3,2},{4,3},{5,4},{6,5},{7,6},{9,8},{10,9},{11,10},{12... | collective-permute-start | bytes 122888 | tf_op jit(solution)/shard_map/ppermute | solution.py:16
  423.8 27.8 %collective-permute-start.16 = (f32[64,128]{1,0:T(8,128)}, f32[64,128]{1,0:T(8,128)S(1)}, u32[]{:S(2)}, u32[]{:S(2)}) collective-permute-start(f32[64,128]{1,0:T(8,128)} %get-tuple-element.28), channel_id=1, source_target_pairs={{0,72},{8,80},{16,88},{24,96},{32,104},{40,112},{48,120},{56,128},... | collective-permute-start | bytes 98312
  425.1 36.0 %collective-permute-start.15 = (f32[64,128]{1,0:T(8,128)}, f32[64,128]{1,0:T(8,128)S(1)}, u32[]{:S(2)}, u32[]{:S(2)}) collective-permute-start(f32[64,128]{1,0:T(8,128)} %get-tuple-element.28), channel_id=1, source_target_pairs={{0,64},{8,72},{16,80},{24,88},{32,96},{40,104},{48,112},{56,120},{... | collective-permute-start | bytes 98312
  426.4 37.9 %collective-permute-start.14 = (f32[64,128]{1,0:T(8,128)}, f32[64,128]{1,0:T(8,128)S(1)}, u32[]{:S(2)}, u32[]{:S(2)}) collective-permute-start(f32[64,128]{1,0:T(8,128)} %get-tuple-element.28), channel_id=1, source_target_pairs={{0,56},{8,64},{16,72},{24,80},{32,88},{40,96},{48,104},{56,112},{6... | collective-permute-start | bytes 98312
  431.2 41.1 %collective-permute-start.13 = (f32[64,128]{1,0:T(8,128)}, f32[64,128]{1,0:T(8,128)S(1)}, u32[]{:S(2)}, u32[]{:S(2)}) collective-permute-start(f32[64,128]{1,0:T(8,128)} %get-tuple-element.28), channel_id=1, source_target_pairs={{0,48},{8,56},{16,64},{24,72},{32,80},{40,88},{48,96},{56,104},{64... | collective-permute-start | bytes 98312
  446.6 27.5 %collective-permute-start.12 = (f32[64,128]{1,0:T(8,128)}, f32[64,128]{1,0:T(8,128)S(1)}, u32[]{:S(2)}, u32[]{:S(2)}) collective-permute-start(f32[64,128]{1,0:T(8,128)} %get-tuple-element.28), channel_id=1, source_target_pairs={{0,40},{8,48},{16,56},{24,64},{32,72},{40,80},{48,88},{56,96},{64,... | collective-permute-start | bytes 98312
  451.6 23.9 %collective-permute-start.11 = (f32[64,128]{1,0:T(8,128)}, f32[64,128]{1,0:T(8,128)S(1)}, u32[]{:S(2)}, u32[]{:S(2)}) collective-permute-start(f32[64,128]{1,0:T(8,128)} %get-tuple-element.28), channel_id=1, source_target_pairs={{0,32},{8,40},{16,48},{24,56},{32,64},{40,72},{48,80},{56,88},{64,... | collective-permute-start | bytes 98312
  461.1 17.9 %collective-permute-start.10 = (f32[64,128]{1,0:T(8,128)}, f32[64,128]{1,0:T(8,128)S(1)}, u32[]{:S(2)}, u32[]{:S(2)}) collective-permute-start(f32[64,128]{1,0:T(8,128)} %get-tuple-element.28), channel_id=1, source_target_pairs={{0,24},{8,32},{16,40},{24,48},{32,56},{40,64},{48,72},{56,80},{64,... | collective-permute-start | bytes 98312
  464.3 18.1 %collective-permute-start.9 = (f32[64,128]{1,0:T(8,128)}, f32[64,128]{1,0:T(8,128)S(1)}, u32[]{:S(2)}, u32[]{:S(2)}) collective-permute-start(f32[64,128]{1,0:T(8,128)} %get-tuple-element.28), channel_id=1, source_target_pairs={{0,16},{8,24},{16,32},{24,40},{32,48},{40,56},{48,64},{56,72},{64,... | collective-permute-start | bytes 98312
  472.2 14.1 %collective-permute-start.8 = (f32[64,128]{1,0:T(8,128)}, f32[64,128]{1,0:T(8,128)S(1)}, u32[]{:S(2)}, u32[]{:S(2)}) collective-permute-start(f32[64,128]{1,0:T(8,128)} %get-tuple-element.28), channel_id=1, source_target_pairs={{0,8},{8,16},{16,24},{24,32},{32,40},{40,48},{48,56},{56,64},{64,7... | collective-permute-start | bytes 98312
  474.2 21.7 %collective-permute-start.26 = (f32[64,128]{1,0:T(8,128)}, f32[64,128]{1,0:T(8,128)S(1)}, u32[]{:S(2)}, u32[]{:S(2)}) collective-permute-start(f32[64,128]{1,0:T(8,128)} %get-tuple-element.29), channel_id=1, source_target_pairs={{0,72},{8,80},{16,88},{24,96},{32,104},{40,112},{48,120},{56,128},... | collective-permute-start | bytes 98312
  475.5 28.2 %collective-permute-start.25 = (f32[64,128]{1,0:T(8,128)}, f32[64,128]{1,0:T(8,128)S(1)}, u32[]{:S(2)}, u32[]{:S(2)}) collective-permute-start(f32[64,128]{1,0:T(8,128)} %get-tuple-element.29), channel_id=1, source_target_pairs={{0,64},{8,72},{16,80},{24,88},{32,96},{40,104},{48,112},{56,120},{... | collective-permute-start | bytes 98312
  479.0 27.1 %collective-permute-start.24 = (f32[64,128]{1,0:T(8,128)}, f32[64,128]{1,0:T(8,128)S(1)}, u32[]{:S(2)}, u32[]{:S(2)}) collective-permute-start(f32[64,128]{1,0:T(8,128)} %get-tuple-element.29), channel_id=1, source_target_pairs={{0,56},{8,64},{16,72},{24,80},{32,88},{40,96},{48,104},{56,112},{6... | collective-permute-start | bytes 98312
  482.4 29.6 %collective-permute-start.23 = (f32[64,128]{1,0:T(8,128)}, f32[64,128]{1,0:T(8,128)S(1)}, u32[]{:S(2)}, u32[]{:S(2)}) collective-permute-start(f32[64,128]{1,0:T(8,128)} %get-tuple-element.29), channel_id=1, source_target_pairs={{0,48},{8,56},{16,64},{24,72},{32,80},{40,88},{48,96},{56,104},{64... | collective-permute-start | bytes 98312
  494.6 20.0 %collective-permute-start.22 = (f32[64,128]{1,0:T(8,128)}, f32[64,128]{1,0:T(8,128)S(1)}, u32[]{:S(2)}, u32[]{:S(2)}) collective-permute-start(f32[64,128]{1,0:T(8,128)} %get-tuple-element.29), channel_id=1, source_target_pairs={{0,40},{8,48},{16,56},{24,64},{32,72},{40,80},{48,88},{56,96},{64,... | collective-permute-start | bytes 98312
  495.9 18.7 %collective-permute-start.21 = (f32[64,128]{1,0:T(8,128)}, f32[64,128]{1,0:T(8,128)S(1)}, u32[]{:S(2)}, u32[]{:S(2)}) collective-permute-start(f32[64,128]{1,0:T(8,128)} %get-tuple-element.29), channel_id=1, source_target_pairs={{0,32},{8,40},{16,48},{24,56},{32,64},{40,72},{48,80},{56,88},{64,... | collective-permute-start | bytes 98312
  503.7 10.9 %collective-permute-start.20 = (f32[64,128]{1,0:T(8,128)}, f32[64,128]{1,0:T(8,128)S(1)}, u32[]{:S(2)}, u32[]{:S(2)}) collective-permute-start(f32[64,128]{1,0:T(8,128)} %get-tuple-element.29), channel_id=1, source_target_pairs={{0,24},{8,32},{16,40},{24,48},{32,56},{40,64},{48,72},{56,80},{64,... | collective-permute-start | bytes 98312
  (13 other events, 142.2 us)
Sparse Core Ops, SparseCore 0:
  185.7 74.0 all-reduce.9
where the time goes:
time: 529 us; the launch traced here: 528 us
  blocking collectives  263 us (50%)
  starting transfers between devices  128 us (24%)
  waiting for transfers between devices  83.3 us (16%)
  between operations  16.3 us (3%)
  local copies, waits for them, and re-layouts  16.2 us (3%)
  matrix products  12.2 us (2%)
  other arithmetic  8.08 us (2%)
    unnamed x1, blocking collectives  163 us
    unnamed x20, starting transfers between devices  82.6 us
    psum x1, waiting for transfers between devices, body(): lax.psum(weight_first.astype(jnp.bfloat16), 'rows').astype(jnp.float32)  74.2 us
    all_gather x1, blocking collectives, body(): lax.all_gather(w_first, 'wide', axis=0, tiled=True)  52.7 us
    all_gather x1, blocking collectives, body(): lax.all_gather(w_second, 'wide', axis=0, tiled=True)  48.3 us
    all_to_all x1, starting transfers between devices, body(): lax.all_to_all(labels, 'wide', split_axis=0, concat_axis=0, tiled=True)  16.4 us
    ppermute x4, starting transfers between devices, with_halo(): lax.ppermute(lax.slice_in_dim(block, block.shape[dim] - width, None, axis...  14.9 us
    unnamed x33, local copies, waits for them, and re-layouts  12.1 us
  transfers between devices with their start and end apart: 31, of which 5 were waited for; matrix products, arithmetic and copies ran while one was open for 4% of the time, Pallas kernels for 0%

commit v1 on v0

--- a/solution.py
+++ b/solution.py
@@ -130,7 +130,9 @@
     weight_first = weight_first * scale
     weight_second = weight_second * scale
     total_first, total_second = (
-        lax.psum(weight_first.astype(jnp.bfloat16), "rows").astype(jnp.float32),
+        jnp.sum(lax.all_gather(weight_first.astype(jnp.bfloat16), axis_name="rows"), axis=0).astype(
+            jnp.float32
+        ),
         lax.psum(weight_second.astype(jnp.bfloat16), "rows").astype(jnp.float32),
     )
     share_first, share_second = (

time: 529 us -> 580 us (1.096)
  waiting for transfers between devices: 83.3 us -> 127 us
  other arithmetic: 8.08 us -> 14.3 us
    all_gather x0 -> x1, waiting for transfers between devices: none -> 49.5 us  [body(): lax.all_gather(weight_first.astype(jnp.bfloat16), axis_name='rows')]
    psum x1, waiting for transfers between devices: 74.2 us -> 68.2 us  [body(): lax.psum(weight_second.astype(jnp.bfloat16), 'rows').astype(jnp.float32)]
    unnamed x33 -> x31, local copies, waits for them, and re-layouts: 12.1 us -> 12 us
  transfers between devices with their start and end apart: 31 -> 32, of which waited for: 5 -> 6; matrix products, arithmetic and copies ran while one was open for 4% -> 4% of each run, Pallas kernels for 0% -> 0%
where the time goes in v1:
time: 580 us; the launch traced here: 578 us
  blocking collectives  263 us (45%)
  starting transfers between devices  129 us (22%)
  waiting for transfers between devices  127 us (22%)
  between operations  16.3 us (3%)
  local copies, waits for them, and re-layouts  16.1 us (3%)
  other arithmetic  14.3 us (2%)
  matrix products  12.2 us (2%)
    unnamed x1, blocking collectives  162 us
    unnamed x20, starting transfers between devices  83.5 us
    psum x1, waiting for transfers between devices, body(): lax.psum(weight_second.astype(jnp.bfloat16), 'rows').astype(jnp.float32)  68.2 us
    all_gather x1, blocking collectives, body(): lax.all_gather(w_first, 'wide', axis=0, tiled=True)  52.7 us
    all_gather x1, waiting for transfers between devices, body(): lax.all_gather(weight_first.astype(jnp.bfloat16), axis_name='rows')  49.5 us
    all_gather x1, blocking collectives, body(): lax.all_gather(w_second, 'wide', axis=0, tiled=True)  48.3 us
    all_to_all x1, starting transfers between devices, body(): lax.all_to_all(labels, 'wide', split_axis=0, concat_axis=0, tiled=True)  16.4 us
    ppermute x4, starting transfers between devices, with_halo(): lax.ppermute(lax.slice_in_dim(block, block.shape[dim] - width, None, axis...  14.9 us
  transfers between devices with their start and end apart: 32, of which 6 were waited for; matrix products, arithmetic and copies ran while one was open for 4% of the time, Pallas kernels for 0%

profile of v1, /device:TPU:24, one launch (start us, length us, event | category | flops | bytes accessed | tf_op | source)
XLA Modules:
  0.0 578.1 jit_solution(15291778664874072127)
XLA Ops:
  10.2 16.4 %all-to-all-start = ((s32[64,1,1]{2,1,0:T(1,128)}), s32[64,1,1]{2,1,0:T(1,128)S(1)}, u32[]{:S(2)}, u32[]{:S(2)}) async-start(s32[64,1,1]{2,1,0:T(1,128)} %copy.172), calls=%async_computation | async-start | bytes 65536 | tf_op jit(solution)/shard_map/all_to_all | solution.py:92
  32.3 3.5 all-to-all-done
  35.8 9.2 %all-to-all-start.1 = ((bf16[64,2,2048]{2,1,0:T(2,128)(2,1)}), bf16[64,2,2048]{2,1,0:T(2,128)(2,1)S(1)}, u32[]{:S(2)}, u32[]{:S(2)}) async-start(bf16[64,2,2048]{2,1,0:T(2,128)(2,1)} %reshape.289), calls=%async_computation.1 | async-start | bytes 1048576 | tf_op jit(solution)/shard_map/all_to_all | solution.py:91
  49.4 52.7 %all-gather = bf16[64,54,128]{2,1,0:T(8,128)(2,1)S(1)} all-gather(bf16[1,54,128]{2,1,0:T(8,128)(2,1)S(1)} %bitcast.138), channel_id=1, replica_groups=mesh['wide'=64,'rows'=8] {'wide'}, dimensions={0}, use_global_device_ids=true | all-gather | bytes 898560 | tf_op jit(solution)/shard_map/all_gather | solution.py:105
  102.1 48.3 %all-gather.1 = bf16[64,54,128]{2,1,0:T(8,128)(2,1)S(1)} all-gather(bf16[1,54,128]{2,1,0:T(8,128)(2,1)S(1)} %bitcast.139), channel_id=1, replica_groups=mesh['wide'=64,'rows'=8] {'wide'}, dimensions={0}, use_global_device_ids=true | all-gather | bytes 898560 | tf_op jit(solution)/shard_map/all_gather | solution.py:106
  164.2 3.8 collective-permute-start.6
  169.3 5.0 collective-permute-start.2
  178.6 3.5 multiply_convert_fusion
  182.1 3.5 multiply_convert_fusion.1
  185.7 68.2 %all-reduce.9.cloned.1.call-done = bf16[3456,128]{1,0:T(8,128)(2,1)} async-done(((bf16[3456,128]{1,0:T(8,128)(2,1)}), bf16[3456,128]{1,0:T(8,128)(2,1)}) %all-reduce.9.cloned.1.call-update) | async-done | bytes 884752 | tf_op jit(solution)/shard_map/psum | solution.py:136
  255.1 49.5 %all-gather.4.cloned.1.call-done = bf16[8,3456,128]{2,1,0:T(8,128)(2,1)} async-done(((bf16[1,3456,128]{2,1,0:T(8,128)(2,1)}), bf16[8,3456,128]{2,1,0:T(8,128)(2,1)}) %all-gather.4.cloned.1.call-update) | async-done | bytes 7077904 | tf_op jit(solution)/shard_map/all_gather | solution.py:133
  304.6 5.2 reduce_sum.32
  311.1 162.1 %fusion.84 = (f32[64,128]{1,0:T(8,128)}, f32[64,128]{1,0:T(8,128)}) fusion(f32[3456,128]{1,0:T(8,128)S(1)} %convert_element_type.122, f32[3456,128]{1,0:T(8,128)S(1)} %convert_element_type.125), kind=kCustom, calls=%all-reduce-scatter.2 | all-reduce-scatter fusion | flops 1048577 | bytes 3606528
  475.8 3.6 collective-permute-start.14
  480.2 12.2 %collective-permute-start.13 = (f32[64,128]{1,0:T(8,128)}, f32[64,128]{1,0:T(8,128)S(1)}, u32[]{:S(2)}, u32[]{:S(2)}) collective-permute-start(f32[64,128]{1,0:T(8,128)} %get-tuple-element.26), channel_id=1, source_target_pairs={{0,48},{8,56},{16,64},{24,72},{32,80},{40,88},{48,96},{56,104},{64... | collective-permute-start | bytes 98312
  495.7 4.9 collective-permute-start.12
  500.6 9.3 %collective-permute-start.11 = (f32[64,128]{1,0:T(8,128)}, f32[64,128]{1,0:T(8,128)S(1)}, u32[]{:S(2)}, u32[]{:S(2)}) collective-permute-start(f32[64,128]{1,0:T(8,128)} %get-tuple-element.26), channel_id=1, source_target_pairs={{0,32},{8,40},{16,48},{24,56},{32,64},{40,72},{48,80},{56,88},{64,... | collective-permute-start | bytes 98312
  509.9 3.4 collective-permute-start.10
  513.3 7.9 %collective-permute-start.9 = (f32[64,128]{1,0:T(8,128)}, f32[64,128]{1,0:T(8,128)S(1)}, u32[]{:S(2)}, u32[]{:S(2)}) collective-permute-start(f32[64,128]{1,0:T(8,128)} %get-tuple-element.26), channel_id=1, source_target_pairs={{0,16},{8,24},{16,32},{24,40},{32,48},{40,56},{48,64},{56,72},{64,... | collective-permute-start | bytes 98312
  524.5 4.8 collective-permute-start.25
  536.7 4.0 collective-permute-start.27
  546.2 7.8 %collective-permute-start.21 = (f32[64,128]{1,0:T(8,128)}, f32[64,128]{1,0:T(8,128)S(1)}, u32[]{:S(2)}, u32[]{:S(2)}) collective-permute-start(f32[64,128]{1,0:T(8,128)} %get-tuple-element.27), channel_id=1, source_target_pairs={{0,32},{8,40},{16,48},{24,56},{32,64},{40,72},{48,80},{56,88},{64,... | collective-permute-start | bytes 98312
  556.5 5.9 %collective-permute-start.19 = (f32[64,128]{1,0:T(8,128)}, f32[64,128]{1,0:T(8,128)S(1)}, u32[]{:S(2)}, u32[]{:S(2)}) collective-permute-start(f32[64,128]{1,0:T(8,128)} %get-tuple-element.27), channel_id=1, source_target_pairs={{0,16},{8,24},{16,32},{24,40},{32,48},{40,56},{48,64},{56,72},{64,... | collective-permute-start | bytes 98312
  565.0 3.4 collective-permute-done.18
  (144 shorter events, 63.7 us)
Async XLA Ops:
  10.2 25.6 %all-to-all-start = ((s32[64,1,1]{2,1,0:T(1,128)}), s32[64,1,1]{2,1,0:T(1,128)S(1)}, u32[]{:S(2)}, u32[]{:S(2)}) async-start(s32[64,1,1]{2,1,0:T(1,128)} %copy.172), calls=%async_computation | async-start | bytes 65536 | tf_op jit(solution)/shard_map/all_to_all | solution.py:92
  35.8 118.9 %all-to-all-start.1 = ((bf16[64,2,2048]{2,1,0:T(2,128)(2,1)}), bf16[64,2,2048]{2,1,0:T(2,128)(2,1)S(1)}, u32[]{:S(2)}, u32[]{:S(2)}) async-start(bf16[64,2,2048]{2,1,0:T(2,128)(2,1)} %reshape.289), calls=%async_computation.1 | async-start | bytes 1048576 | tf_op jit(solution)/shard_map/all_to_all | solution.py:91
  45.0 208.8 %all-reduce.9.cloned.1.call-start = ((), (), s32[]{:S(2)}) async-start(), calls=%async_computation.3 | async-start | bytes 1769472 | tf_op jit(solution)/shard_map/psum | solution.py:136
  45.1 107.9 %collective-permute-start.5 = (bf16[5,1,32,128]{3,2,1,0:T(8,128)(2,1)S(1)}, bf16[5,1,32,128]{3,2,1,0:T(8,128)(2,1)S(1)}, u32[]{:S(2)}, u32[]{:S(2)}) collective-permute-start(bf16[5,1,32,128]{3,2,1,0:T(8,128)(2,1)S(1)} %get-tuple-element.42), channel_id=1, source_target_pairs={{1,0},{2,1},{3,2},{4,3},{5,4},{6,5},{7,6},{9,8},{10,9},{11,10},{12... | collective-permute-start | bytes 122888 | tf_op jit(solution)/shard_map/ppermute | solution.py:16
  46.4 106.6 %collective-permute-start.4 = (bf16[5,1,32,128]{3,2,1,0:T(8,128)(2,1)S(1)}, bf16[5,1,32,128]{3,2,1,0:T(8,128)(2,1)S(1)}, u32[]{:S(2)}, u32[]{:S(2)}) collective-permute-start(bf16[5,1,32,128]{3,2,1,0:T(8,128)(2,1)S(1)} %get-tuple-element.41), channel_id=1, source_target_pairs={{0,1},{1,2},{2,3},{3,4},{4,5},{5,6},{6,7},{8,9},{9,10},{10,11},{11... | collective-permute-start | bytes 122888 | tf_op jit(solution)/shard_map/ppermute | solution.py:13
  162.9 11.6 %collective-permute-start.7 = (bf16[5,1,32,128]{3,2,1,0:T(8,128)(2,1)S(1)}, bf16[5,1,32,128]{3,2,1,0:T(8,128)(2,1)S(1)}, u32[]{:S(2)}, u32[]{:S(2)}) collective-permute-start(bf16[5,1,32,128]{3,2,1,0:T(8,128)(2,1)S(1)} %get-tuple-element.38), channel_id=1, source_target_pairs={{1,0},{2,1},{3,2},{4,3},{5,4},{6,5},{7,6},{9,8},{10,9},{11,10},{12... | collective-permute-start | bytes 122888 | tf_op jit(solution)/shard_map/ppermute | solution.py:16
  164.2 10.3 %collective-permute-start.6 = (bf16[5,1,32,128]{3,2,1,0:T(8,128)(2,1)S(1)}, bf16[5,1,32,128]{3,2,1,0:T(8,128)(2,1)S(1)}, u32[]{:S(2)}, u32[]{:S(2)}) collective-permute-start(bf16[5,1,32,128]{3,2,1,0:T(8,128)(2,1)S(1)} %get-tuple-element.37), channel_id=1, source_target_pairs={{0,1},{1,2},{2,3},{3,4},{4,5},{5,6},{6,7},{8,9},{9,10},{10,11},{11... | collective-permute-start | bytes 122888 | tf_op jit(solution)/shard_map/ppermute | solution.py:13
  182.1 122.5 %all-gather.4.cloned.1.call-start = ((), (), s32[]{:S(2)}) async-start(), calls=%async_computation.2 | async-start | bytes 7962624 | tf_op jit(solution)/shard_map/all_gather | solution.py:133
  473.2 27.4 %collective-permute-start.16 = (f32[64,128]{1,0:T(8,128)}, f32[64,128]{1,0:T(8,128)S(1)}, u32[]{:S(2)}, u32[]{:S(2)}) collective-permute-start(f32[64,128]{1,0:T(8,128)} %get-tuple-element.26), channel_id=1, source_target_pairs={{0,72},{8,80},{16,88},{24,96},{32,104},{40,112},{48,120},{56,128},... | collective-permute-start | bytes 98312
  474.5 35.4 %collective-permute-start.15 = (f32[64,128]{1,0:T(8,128)}, f32[64,128]{1,0:T(8,128)S(1)}, u32[]{:S(2)}, u32[]{:S(2)}) collective-permute-start(f32[64,128]{1,0:T(8,128)} %get-tuple-element.26), channel_id=1, source_target_pairs={{0,64},{8,72},{16,80},{24,88},{32,96},{40,104},{48,112},{56,120},{... | collective-permute-start | bytes 98312
  475.8 37.5 %collective-permute-start.14 = (f32[64,128]{1,0:T(8,128)}, f32[64,128]{1,0:T(8,128)S(1)}, u32[]{:S(2)}, u32[]{:S(2)}) collective-permute-start(f32[64,128]{1,0:T(8,128)} %get-tuple-element.26), channel_id=1, source_target_pairs={{0,56},{8,64},{16,72},{24,80},{32,88},{40,96},{48,104},{56,112},{6... | collective-permute-start | bytes 98312
  480.2 41.1 %collective-permute-start.13 = (f32[64,128]{1,0:T(8,128)}, f32[64,128]{1,0:T(8,128)S(1)}, u32[]{:S(2)}, u32[]{:S(2)}) collective-permute-start(f32[64,128]{1,0:T(8,128)} %get-tuple-element.26), channel_id=1, source_target_pairs={{0,48},{8,56},{16,64},{24,72},{32,80},{40,88},{48,96},{56,104},{64... | collective-permute-start | bytes 98312
  495.7 27.5 %collective-permute-start.12 = (f32[64,128]{1,0:T(8,128)}, f32[64,128]{1,0:T(8,128)S(1)}, u32[]{:S(2)}, u32[]{:S(2)}) collective-permute-start(f32[64,128]{1,0:T(8,128)} %get-tuple-element.26), channel_id=1, source_target_pairs={{0,40},{8,48},{16,56},{24,64},{32,72},{40,80},{48,88},{56,96},{64,... | collective-permute-start | bytes 98312
  500.6 23.9 %collective-permute-start.11 = (f32[64,128]{1,0:T(8,128)}, f32[64,128]{1,0:T(8,128)S(1)}, u32[]{:S(2)}, u32[]{:S(2)}) collective-permute-start(f32[64,128]{1,0:T(8,128)} %get-tuple-element.26), channel_id=1, source_target_pairs={{0,32},{8,40},{16,48},{24,56},{32,64},{40,72},{48,80},{56,88},{64,... | collective-permute-start | bytes 98312
  509.9 19.5 %collective-permute-start.10 = (f32[64,128]{1,0:T(8,128)}, f32[64,128]{1,0:T(8,128)S(1)}, u32[]{:S(2)}, u32[]{:S(2)}) collective-permute-start(f32[64,128]{1,0:T(8,128)} %get-tuple-element.26), channel_id=1, source_target_pairs={{0,24},{8,32},{16,40},{24,48},{32,56},{40,64},{48,72},{56,80},{64,... | collective-permute-start | bytes 98312
  513.3 19.4 %collective-permute-start.9 = (f32[64,128]{1,0:T(8,128)}, f32[64,128]{1,0:T(8,128)S(1)}, u32[]{:S(2)}, u32[]{:S(2)}) collective-permute-start(f32[64,128]{1,0:T(8,128)} %get-tuple-element.26), channel_id=1, source_target_pairs={{0,16},{8,24},{16,32},{24,40},{32,48},{40,56},{48,64},{56,72},{64,... | collective-permute-start | bytes 98312
  521.3 15.4 %collective-permute-start.8 = (f32[64,128]{1,0:T(8,128)}, f32[64,128]{1,0:T(8,128)S(1)}, u32[]{:S(2)}, u32[]{:S(2)}) collective-permute-start(f32[64,128]{1,0:T(8,128)} %get-tuple-element.26), channel_id=1, source_target_pairs={{0,8},{8,16},{16,24},{24,32},{32,40},{40,48},{48,56},{56,64},{64,7... | collective-permute-start | bytes 98312
  523.2 23.0 %collective-permute-start.26 = (f32[64,128]{1,0:T(8,128)}, f32[64,128]{1,0:T(8,128)S(1)}, u32[]{:S(2)}, u32[]{:S(2)}) collective-permute-start(f32[64,128]{1,0:T(8,128)} %get-tuple-element.27), channel_id=1, source_target_pairs={{0,72},{8,80},{16,88},{24,96},{32,104},{40,112},{48,120},{56,128},... | collective-permute-start | bytes 98312
  524.5 29.5 %collective-permute-start.25 = (f32[64,128]{1,0:T(8,128)}, f32[64,128]{1,0:T(8,128)S(1)}, u32[]{:S(2)}, u32[]{:S(2)}) collective-permute-start(f32[64,128]{1,0:T(8,128)} %get-tuple-element.27), channel_id=1, source_target_pairs={{0,64},{8,72},{16,80},{24,88},{32,96},{40,104},{48,112},{56,120},{... | collective-permute-start | bytes 98312
  529.4 27.1 %collective-permute-start.24 = (f32[64,128]{1,0:T(8,128)}, f32[64,128]{1,0:T(8,128)S(1)}, u32[]{:S(2)}, u32[]{:S(2)}) collective-permute-start(f32[64,128]{1,0:T(8,128)} %get-tuple-element.27), channel_id=1, source_target_pairs={{0,56},{8,64},{16,72},{24,80},{32,88},{40,96},{48,104},{56,112},{6... | collective-permute-start | bytes 98312
  532.8 29.6 %collective-permute-start.23 = (f32[64,128]{1,0:T(8,128)}, f32[64,128]{1,0:T(8,128)S(1)}, u32[]{:S(2)}, u32[]{:S(2)}) collective-permute-start(f32[64,128]{1,0:T(8,128)} %get-tuple-element.27), channel_id=1, source_target_pairs={{0,48},{8,56},{16,64},{24,72},{32,80},{40,88},{48,96},{56,104},{64... | collective-permute-start | bytes 98312
  544.9 20.0 %collective-permute-start.22 = (f32[64,128]{1,0:T(8,128)}, f32[64,128]{1,0:T(8,128)S(1)}, u32[]{:S(2)}, u32[]{:S(2)}) collective-permute-start(f32[64,128]{1,0:T(8,128)} %get-tuple-element.27), channel_id=1, source_target_pairs={{0,40},{8,48},{16,56},{24,64},{32,72},{40,80},{48,88},{56,96},{64,... | collective-permute-start | bytes 98312
  546.2 18.7 %collective-permute-start.21 = (f32[64,128]{1,0:T(8,128)}, f32[64,128]{1,0:T(8,128)S(1)}, u32[]{:S(2)}, u32[]{:S(2)}) collective-permute-start(f32[64,128]{1,0:T(8,128)} %get-tuple-element.27), channel_id=1, source_target_pairs={{0,32},{8,40},{16,48},{24,56},{32,64},{40,72},{48,80},{56,88},{64,... | collective-permute-start | bytes 98312
  554.0 10.9 %collective-permute-start.20 = (f32[64,128]{1,0:T(8,128)}, f32[64,128]{1,0:T(8,128)S(1)}, u32[]{:S(2)}, u32[]{:S(2)}) collective-permute-start(f32[64,128]{1,0:T(8,128)} %get-tuple-element.27), channel_id=1, source_target_pairs={{0,24},{8,32},{16,40},{24,48},{32,56},{40,64},{48,72},{56,80},{64,... | collective-permute-start | bytes 98312
  (13 other events, 144.6 us)
Sparse Core Ops, SparseCore 0:
  182.2 71.5 all-reduce.8
  256.2 48.4 all-gather.3
